TPU v7x, 32 devices: a whole 2x2x4 slice. The times are simulated.
32 devices in a mesh: seq: 4 (over x, core), mp: 8 (over z, y).
Axes of the slice: x: 2, y: 2, z: 4, core: 2. Of those that a mesh axis runs over, the one named last changes fastest.
Arguments:
- tokens: bfloat16 [2, 6144, 1024], P(None, ('seq', 'mp')), may hold values from -6 to 6
- ln1_gain: float32 [1024], replicated, may hold values from 0.1 to 1.9
- ln1_bias: float32 [1024], replicated, may hold values from -1.75 to 1.75
- ln2_gain: float32 [1024], replicated, may hold values from 0.1 to 1.9
- ln2_bias: float32 [1024], replicated, may hold values from -1.75 to 1.75
- q_weight: bfloat16 [1024, 1024], P('seq', 'mp'), may hold values from -0.1875 to 0.1875
- k_weight: bfloat16 [1024, 1024], P('seq', 'mp'), may hold values from -0.1875 to 0.1875
- value_weight: bfloat16 [1024, 1024], P('seq', 'mp'), may hold values from -0.1875 to 0.1875
- out_weight: bfloat16 [1024, 1024], P('mp', 'seq'), may hold values from -2 to 2
- up_weight: bfloat16 [1024, 4096], P('seq', 'mp'), may hold values from -0.1875 to 0.1875
- down_weight: bfloat16 [4096, 1024], P('mp', 'seq'), may hold values from -0.09375 to 0.09375
- lengths: int32 [2, 4, 3], P(None, 'seq'), may hold values from 1 to 1024, 1536 in all within a row
- cotangent: bfloat16 [2, 6144, 1024], P(None, ('seq', 'mp')), may hold values from -12 to 12
Outputs:
- mixed: bfloat16 [2, 6144, 1024], P(None, ('seq', 'mp'))
- grad_tokens: float32 [2, 6144, 1024], P(None, ('seq', 'mp'))
- grad_ln1_gain: float32 [1024], replicated
- grad_ln1_bias: float32 [1024], replicated
- grad_ln2_gain: float32 [1024], replicated
- grad_ln2_bias: float32 [1024], replicated
- grad_q_weight: float32 [1024, 1024], P('seq', 'mp')
- grad_k_weight: float32 [1024, 1024], P('seq', 'mp')
- grad_v_weight: float32 [1024, 1024], P('seq', 'mp')
- grad_out_weight: float32 [1024, 1024], P('mp', 'seq')
- grad_up_weight: float32 [1024, 4096], P('seq', 'mp')
- grad_down_weight: float32 [4096, 1024], P('mp', 'seq')
Inputs may be any that keep to these rules, and one draw needn't show every extreme that they name: lengths[m, s] lists the 3 documents of row group s of micro-batch m in order; each row sums to 1536, and its longest document holds exactly 1024 tokens.
All inputs are finite; a program needn't handle non-finite values.
Results may differ from a plain program's by a relative error of at most 0.013.
Values may be sent and summed in bfloat16 or wider, within the bound.
No kernel may reach another device: no remote copies, remote signals or barrier semaphores. Data moves between devices by JAX's collectives and lax.ppermute only.
A program may use at most 192 MiB of HBM per device.

v0:
```python
from functools import partial
import math
import jax
import jax.numpy as jnp
from jax import lax
from jax.sharding import PartitionSpec as P

HEAD_DIM = 64
ROT = 16
FEATS = 64


def prime_list(wanted):
    found_primes = []
    candidate = 2
    while len(found_primes) < wanted:
        if all((candidate % earlier != 0 for earlier in found_primes)):
            found_primes.append(candidate)
        candidate += 1
    return found_primes


def feature_maps(head_width, feature_count):
    primes_found = prime_list(head_width)
    uniform_rows = [
        [
            min(max((row_idx + 0.5) * math.sqrt(prime_val) % 1.0, 0.001), 0.999)
            for prime_val in primes_found
        ]
        for row_idx in range(feature_count)
    ]
    uniform_pts = jnp.asarray(uniform_rows, jnp.float32)
    points = math.sqrt(2.0) * lax.erf_inv(2.0 * uniform_pts - 1.0)
    cosine_rows = [
        [
            math.sqrt(2.0 / head_width)
            * math.cos(math.pi * (cell_idx + 0.5) * freq_idx / head_width)
            * (math.sqrt(0.5) if freq_idx == 0 else 1.0)
            for cell_idx in range(head_width)
        ]
        for freq_idx in range(head_width)
    ]
    cosine = jnp.asarray(cosine_rows, jnp.float32)
    project = jnp.dot(points, cosine, precision=lax.Precision.HIGHEST)
    project = jnp.transpose(project) * (1.0 / math.sqrt(head_width))
    weighting = 1.0 / (1.0 + jnp.sum(points * points, axis=1) / head_width)
    return (project, weighting)


def rotate_heads(values, offset):
    half_dims = ROT // 2
    inverse = 10000.0 ** (-jnp.arange(half_dims, dtype=jnp.float32) * 2.0 / ROT)
    angles = offset[:, None] * inverse[None, :]
    cosine = jnp.cos(angles)[None, :, :]
    sine_part = jnp.sin(angles)[None, :, :]
    first_half = values[..., :half_dims]
    second = values[..., half_dims:ROT]
    return jnp.concatenate(
        [
            first_half * cosine - second * sine_part,
            second * cosine + first_half * sine_part,
            values[..., ROT:],
        ],
        axis=-1,
    )


def layer_norm(values, gain_vec, bias_vec):
    centered = values - jnp.mean(values, axis=-1, keepdims=True)
    variance = jnp.mean(centered * centered, axis=-1, keepdims=True)
    return centered * lax.rsqrt(variance + 1e-05) * gain_vec + bias_vec


def exact_gelu(values):
    return jax.nn.gelu(values, approximate=False)


def doc_layout(doc_lengths, number_of_tokens):
    doc_ends = jnp.cumsum(doc_lengths).astype(jnp.int32)
    starts = (doc_ends - doc_lengths).astype(jnp.int32)
    places = jnp.arange(number_of_tokens, dtype=jnp.int32)
    segment = jnp.sum((places[:, None] >= doc_ends[None, :]).astype(jnp.int32), axis=1).astype(
        jnp.int32
    )
    member = segment[:, None] == jnp.arange(doc_lengths.shape[0], dtype=jnp.int32)[None, :]
    offset = places - jnp.sum(jnp.where(member, starts[None, :], 0), axis=1).astype(jnp.int32)
    return (segment, offset.astype(jnp.float32))


def contract_rows(left_side, right_side):
    return lax.dot_general(
        left_side, right_side, (((0,), (0,)), ((), ())), preferred_element_type=jnp.float32
    )


def contract_cols(left_side, right_side):
    return lax.dot_general(
        left_side, right_side, (((1,), (1,)), ((), ())), preferred_element_type=jnp.float32
    )


def local_attention(plain_query_rows, key_raw, value_raw, segment, offset, project, weighting):
    maximal_precision_mode = lax.Precision.HIGHEST
    number_of_tokens = plain_query_rows.shape[0]
    head_count = plain_query_rows.shape[1] // HEAD_DIM

    def heads_first(values):
        return jnp.transpose(values.reshape(number_of_tokens, head_count, HEAD_DIM), (1, 0, 2))

    rot_query = rotate_heads(heads_first(plain_query_rows), offset)
    rot_key = rotate_heads(heads_first(key_raw), offset)
    value_heads = heads_first(value_raw)
    feat_query = (
        jnp.exp(jnp.einsum("htd,df->htf", rot_query, project, precision=maximal_precision_mode))
        * weighting
    )
    feat_key = jnp.exp(
        jnp.einsum("htd,df->htf", rot_key, project, precision=maximal_precision_mode)
    )
    rows_per_block = min(512, number_of_tokens)
    block_count = number_of_tokens // rows_per_block

    def split_blocks(values):
        return jnp.transpose(
            values.reshape((head_count, block_count, rows_per_block, values.shape[2])), (1, 0, 2, 3)
        )

    def block_step(carry, pieces):
        kv_state, totals, previous = carry
        block_of_queries, block_of_keys, value_block, block_segment = pieces
        places = jnp.arange(block_segment.shape[0], dtype=jnp.int32)
        attention_scores = jnp.einsum(
            "ugy,uky->ugk", block_of_queries, block_of_keys, precision=maximal_precision_mode
        )
        allowed = (places[:, None] >= places[None, :]) & (
            block_segment[:, None] == block_segment[None, :]
        )
        attention_scores = jnp.where(allowed[None, :, :], attention_scores, 0.0)
        numerator = jnp.einsum(
            "hqk,hkd->hqd", attention_scores, value_block, precision=maximal_precision_mode
        )
        denominator = jnp.sum(attention_scores, axis=2)
        carried_in = (block_segment == previous)[None, :]
        numerator = numerator + jnp.where(
            carried_in[:, :, None],
            jnp.einsum(
                "hqf,hfd->hqd", block_of_queries, kv_state, precision=maximal_precision_mode
            ),
            0.0,
        )
        denominator = denominator + jnp.where(
            carried_in,
            jnp.einsum("hqf,hf->hq", block_of_queries, totals, precision=maximal_precision_mode),
            0.0,
        )
        final_output = block_segment[-1]
        carried_over = final_output == previous
        trailing_mask = (block_segment == final_output).astype(jnp.float32)
        new_state = jnp.where(carried_over, kv_state, 0.0) + jnp.einsum(
            "hrf,hrd,r->hfd",
            block_of_keys,
            value_block,
            trailing_mask,
            precision=maximal_precision_mode,
        )
        new_totals = jnp.where(carried_over, totals, 0.0) + jnp.einsum(
            "hrf,r->hf", block_of_keys, trailing_mask, precision=maximal_precision_mode
        )
        return ((new_state, new_totals, final_output), numerator / denominator[:, :, None])

    start_carry = (
        jnp.zeros((head_count, FEATS, HEAD_DIM), jnp.float32),
        jnp.zeros((head_count, FEATS), jnp.float32),
        jnp.array(-1, jnp.int32),
    )
    _, outputs = lax.scan(
        jax.checkpoint(block_step),
        start_carry,
        (
            split_blocks(feat_query),
            split_blocks(feat_key),
            split_blocks(value_heads),
            segment.reshape(block_count, rows_per_block),
        ),
    )
    joined = jnp.transpose(outputs, (1, 0, 2, 3)).reshape(head_count, number_of_tokens, HEAD_DIM)
    return jnp.transpose(joined, (1, 0, 2)).reshape(number_of_tokens, head_count * HEAD_DIM)


def local(
    tokens,
    ln1_gain,
    ln1_bias,
    ln2_gain,
    ln2_bias,
    q_weight,
    k_weight,
    value_weight,
    out_weight,
    up_weight,
    down_weight,
    lengths,
    cotangent,
):
    micro_count = tokens.shape[0]
    local_rows = tokens.shape[1]
    group_rows = local_rows * lax.axis_size("mp")
    seq_count = lax.axis_size("seq")
    project, weighting = feature_maps(HEAD_DIM, FEATS)
    grad_sums = [
        jnp.zeros((q_weight.shape[0] * seq_count, q_weight.shape[1]), jnp.float32),
        jnp.zeros((k_weight.shape[0] * seq_count, k_weight.shape[1]), jnp.float32),
        jnp.zeros((value_weight.shape[0] * seq_count, value_weight.shape[1]), jnp.float32),
        jnp.zeros((out_weight.shape[0], out_weight.shape[1] * seq_count), jnp.float32),
        jnp.zeros((up_weight.shape[0] * seq_count, up_weight.shape[1]), jnp.float32),
        jnp.zeros((down_weight.shape[0], down_weight.shape[1] * seq_count), jnp.float32),
    ]
    norm_sums = [
        jnp.zeros_like(ln1_gain),
        jnp.zeros_like(ln1_bias),
        jnp.zeros_like(ln2_gain),
        jnp.zeros_like(ln2_bias),
    ]
    mixed_parts = []
    grad_parts = []
    for micro_step in range(micro_count):
        full_weights = (
            lax.all_gather(q_weight, "seq", axis=0, tiled=True),
            lax.all_gather(k_weight, "seq", axis=0, tiled=True),
            lax.all_gather(value_weight, "seq", axis=0, tiled=True),
            lax.all_gather(out_weight, "seq", axis=1, tiled=True),
            lax.all_gather(up_weight, "seq", axis=0, tiled=True),
            lax.all_gather(down_weight, "seq", axis=1, tiled=True),
        )
        w_query, w_key, w_value, w_out, w_up, w_down = full_weights
        rows_in = tokens[micro_step].astype(jnp.float32)
        normed_one, pull_one = jax.vjp(layer_norm, rows_in, ln1_gain, ln1_bias)
        normed_two, pull_two = jax.vjp(layer_norm, rows_in, ln2_gain, ln2_bias)
        group_one, group_two = (
            lax.all_gather(normed_one.astype(jnp.bfloat16), "mp", axis=0, tiled=True),
            lax.all_gather(normed_two.astype(jnp.bfloat16), "mp", axis=0, tiled=True),
        )
        plain_query_rows = jnp.dot(group_one, w_query, preferred_element_type=jnp.float32)
        key_raw = jnp.dot(group_one, w_key, preferred_element_type=jnp.float32)
        value_raw = jnp.dot(group_one, w_value, preferred_element_type=jnp.float32)
        segment, offset = doc_layout(lengths[micro_step, 0], group_rows)
        attend = partial(
            local_attention, segment=segment, offset=offset, project=project, weighting=weighting
        )
        context, pull_attn = jax.vjp(attend, plain_query_rows, key_raw, value_raw)
        context_low = context.astype(jnp.bfloat16)
        hidden = jnp.dot(group_two, w_up, preferred_element_type=jnp.float32)
        activated, pull_gelu = jax.vjp(exact_gelu, hidden)
        activated_low = activated.astype(jnp.bfloat16)
        context_rows = lax.slice_in_dim(context_low, 0, lax.axis_size("mp") * local_rows, axis=0)
        active_rows = lax.slice_in_dim(activated_low, 0, lax.axis_size("mp") * local_rows, axis=0)
        branch_sum = lax.psum_scatter(
            jnp.dot(context_rows, w_out, preferred_element_type=jnp.float32)
            + jnp.dot(active_rows, w_down, preferred_element_type=jnp.float32),
            "mp",
            scatter_dimension=0,
            tiled=True,
        )
        mixed_parts.append((rows_in + branch_sum).astype(jnp.bfloat16))
        grad_group = lax.all_gather(cotangent[micro_step], "mp", axis=0, tiled=True)
        grad_context = contract_cols(grad_group, w_out)
        grad_activated = contract_cols(grad_group, w_down)
        grad_hidden = pull_gelu(grad_activated)[0].astype(jnp.bfloat16)
        grad_query_f, grad_key_f, grad_value_f = pull_attn(grad_context)
        grad_query = grad_query_f.astype(jnp.bfloat16)
        grad_key = grad_key_f.astype(jnp.bfloat16)
        grad_value = grad_value_f.astype(jnp.bfloat16)
        micro_grads = (
            contract_rows(group_one, grad_query),
            contract_rows(group_one, grad_key),
            contract_rows(group_one, grad_value),
            contract_rows(context_low, grad_group),
            contract_rows(group_two, grad_hidden),
            contract_rows(activated_low, grad_group),
        )
        grad_sums = [total + term for total, term in zip(grad_sums, micro_grads)]
        part_one = (
            contract_cols(grad_query, w_query)
            + contract_cols(grad_key, w_key)
            + contract_cols(grad_value, w_value)
        )
        part_two = contract_cols(grad_hidden, w_up)
        sum_one, sum_two = (
            lax.psum_scatter(
                part_one.astype(jnp.bfloat16), "mp", scatter_dimension=0, tiled=True
            ).astype(jnp.float32),
            lax.psum_scatter(
                part_two.astype(jnp.bfloat16), "mp", scatter_dimension=0, tiled=True
            ).astype(jnp.float32),
        )
        grad_in_one, grad_gain_one, grad_bias_one = pull_one(sum_one)
        grad_in_two, grad_gain_two, grad_bias_two = pull_two(sum_two)
        grad_parts.append(cotangent[micro_step].astype(jnp.float32) + grad_in_one + grad_in_two)
        norm_sums = [
            norm_sums[0] + grad_gain_one,
            norm_sums[1] + grad_bias_one,
            norm_sums[2] + grad_gain_two,
            norm_sums[3] + grad_bias_two,
        ]
    weight_grads = (
        lax.psum_scatter(
            grad_sums[0].astype(jnp.bfloat16), "seq", scatter_dimension=0, tiled=True
        ).astype(jnp.float32),
        lax.psum_scatter(
            grad_sums[1].astype(jnp.bfloat16), "seq", scatter_dimension=0, tiled=True
        ).astype(jnp.float32),
        lax.psum_scatter(
            grad_sums[2].astype(jnp.bfloat16), "seq", scatter_dimension=0, tiled=True
        ).astype(jnp.float32),
        lax.psum_scatter(
            grad_sums[3].astype(jnp.bfloat16), "seq", scatter_dimension=1, tiled=True
        ).astype(jnp.float32),
        lax.psum_scatter(
            grad_sums[4].astype(jnp.bfloat16), "seq", scatter_dimension=0, tiled=True
        ).astype(jnp.float32),
        lax.psum_scatter(
            grad_sums[5].astype(jnp.bfloat16), "seq", scatter_dimension=1, tiled=True
        ).astype(jnp.float32),
    )
    norm_grads = lax.psum((norm_sums[0], norm_sums[1], norm_sums[2], norm_sums[3]), ("seq", "mp"))
    return (
        jnp.stack(mixed_parts),
        jnp.stack(grad_parts),
        norm_grads[0],
        norm_grads[1],
        norm_grads[2],
        norm_grads[3],
        weight_grads[0],
        weight_grads[1],
        weight_grads[2],
        weight_grads[3],
        weight_grads[4],
        weight_grads[5],
    )


def solution(mesh):
    in_specs = (
        P(None, ("seq", "mp"), None),
        P(),
        P(),
        P(),
        P(),
        P("seq", "mp"),
        P("seq", "mp"),
        P("seq", "mp"),
        P("mp", "seq"),
        P("seq", "mp"),
        P("mp", "seq"),
        P(None, "seq", None),
        P(None, ("seq", "mp"), None),
    )
    out_specs = (
        P(None, ("seq", "mp"), None),
        P(None, ("seq", "mp"), None),
        P(),
        P(),
        P(),
        P(),
        P("seq", "mp"),
        P("seq", "mp"),
        P("seq", "mp"),
        P("mp", "seq"),
        P("seq", "mp"),
        P("mp", "seq"),
    )
    return jax.shard_map(local, mesh=mesh, in_specs=in_specs, out_specs=out_specs, check_vma=False)
```

profile of v0, /device:TPU:0, one launch (start us, length us, event | category | flops | bytes accessed | tf_op | source)
XLA Modules:
  0.0 1165.4 jit_solution(13924311496966079492)
XLA Ops:
  20.3 7.7 all_gather.43
  27.9 5.8 all_gather.45
  35.7 5.9 all_gather.44
  41.5 6.3 all_gather.46
  48.9 27.5 %all-gather.19.cloned.1.call-done = bf16[1536,1024]{1,0:T(8,128)(2,1)} async-done(((bf16[192,1024]{1,0:T(8,128)(2,1)}), bf16[1536,1024]{1,0:T(8,128)(2,1)}) %all-gather.19.cloned.1.call-update) | async-done | bytes 3145744 | tf_op jit(solution)/shard_map/all_gather | solution.py:240
  76.4 3.1 fusion.383
  81.2 56.1 %all-gather.11.cloned.1.call-done = bf16[1536,1024]{1,0:T(8,128)(2,1)} async-done(((bf16[192,1024]{1,0:T(8,128)(2,1)}), bf16[1536,1024]{1,0:T(8,128)(2,1)}) %all-gather.11.cloned.1.call-update) | async-done | bytes 3145744 | tf_op jit(solution)/shard_map/all_gather | solution.py:240
  137.3 3.1 fusion.379
  151.1 2.9 reshape.628
  156.4 2.9 convolution_exponential_fusion.1
  170.9 50.6 %while.95 = (s32[]{:T(128)}, f32[2,64,64]{2,1,0:T(8,128)S(1)}, f32[2,64]{1,0:T(2,128)S(1)}, s32[]{:T(128)}, bf16[3,2,512,64]{2,3,1,0:T(8,128)(2,1)}, /*index=5*/...) while((s32[]{:T(128)}, f32[2,64,64]{2,1,0:T(8,128)S(1)}, ...), condition=%wide.region_17.18_spmd.clone, body=%wide.region_15.17_spmd.clone.sunk | while | flops 910208896 | bytes 8145129 | solution.py:176
  172.6 3.0 select_reduce_fusion.11
  178.0 3.3 fusion.628
  189.5 3.0 select_reduce_fusion.11
  194.8 3.3 fusion.628
  206.4 3.0 select_reduce_fusion.11
  211.7 3.3 fusion.628
  221.5 3.1 fusion.240
  228.2 79.3 %while.97 = (s32[]{:T(128)}, f32[2,64,64]{2,1,0:T(8,128)}, f32[2,64]{1,0:T(2,128)S(1)}, f32[3,2,512,64]{2,3,1,0:T(8,128)}, f32[3,2,512,64]{2,3,1,0:T(8,128)}, /*...) while((s32[]{:T(128)}, f32[2,64,64]{2,1,0:T(8,128)}, ...), condition=%wide.region_32.33_spmd.clone, body=%wide.region_29.32_spmd.clone.sunk | while | flops 2675472384 | bytes 24581376 | solution.py:176
  332.6 42.4 %while.94 = (s32[]{:T(128)}, f32[2,64,64]{2,1,0:T(8,128)S(1)}, f32[2,64]{1,0:T(2,128)S(1)}, s32[]{:T(128)}, bf16[3,2,512,64]{2,3,1,0:T(8,128)(2,1)}, /*index=5*/...) while((s32[]{:T(128)}, f32[2,64,64]{2,1,0:T(8,128)S(1)}, ...), condition=%wide.region_8.9_spmd.clone, body=%wide.region_6.8_spmd.clone.sunk | while | flops 910208896 | bytes 8145645 | solution.py:176
  333.1 3.0 select_reduce_fusion.10
  337.9 3.3 fusion.613
  347.2 3.0 select_reduce_fusion.10
  352.0 3.3 fusion.613
  361.4 3.0 select_reduce_fusion.10
  366.2 3.3 fusion.613
  375.0 3.1 fusion.248
  380.6 67.8 %while.96 = (s32[]{:T(128)}, f32[2,64,64]{2,1,0:T(8,128)S(1)}, f32[2,64]{1,0:T(2,128)S(1)}, f32[3,2,512,64]{2,3,1,0:T(8,128)}, f32[3,2,512,64]{2,3,1,0:T(8,128)}...) while((s32[]{:T(128)}, f32[2,64,64]{2,1,0:T(8,128)S(1)}, ...), condition=%wide.region_22.23_spmd.clone, body=%wide.region_19.22_spmd.clone.sunk | while | flops 2675472384 | bytes 24581376 | solution.py:176
  463.1 2.9 fusion.389
  468.6 3.0 fusion.391
  477.8 12.2 %multiply_convert_fusion.1 = (bf16[1536,512]{1,0:T(8,128)(2,1)}, f32[1536,512]{1,0:T(8,128)}, f32[1536,512]{1,0:T(8,128)}) fusion(bf16[1536,1024]{1,0:T(8,128)(2,1)} %all-gather.13.cloned.1.call-done, bf16[1024,512]{1,0:T(8,128)(2,1)} %all-gather.15.cloned.1.call-done), kind=kOutput, calls=%fused_computation.309 | convolution fusion | flops 1661730816 | bytes 12058624 | tf_op jit(solution)/shard_map/dot_general | solution.py:252
  490.0 12.0 %multiply_convert_fusion = (bf16[1536,512]{1,0:T(8,128)(2,1)}, f32[1536,512]{1,0:T(8,128)}, f32[1536,512]{1,0:T(8,128)}) fusion(bf16[1536,1024]{1,0:T(8,128)(2,1)} %all-gather.21.cloned.1.call-done, bf16[1024,512]{1,0:T(8,128)(2,1)} %all-gather.15.cloned.1.call-done), kind=kOutput, calls=%fused_computation.296 | convolution fusion | flops 1661730816 | bytes 12058624 | tf_op jit(solution)/shard_map/dot_general | solution.py:252
  502.0 6.1 add_convert_fusion.3
  516.9 2.8 add_convert_fusion.5
  519.9 4.3 fusion.234
  540.5 3.5 convolution_convert_fusion.1
  545.4 3.5 convolution_convert_fusion
  552.5 3.7 convolution_add_fusion.8
  559.6 3.8 convolution_add_fusion.9
  569.5 5.3 reduce-scatter.33.cloned.1.call-done
  576.6 25.4 %reduce-scatter.35.cloned.1.call-done = bf16[512,256]{1,0:T(8,128)(2,1)} async-done(((bf16[512,1024]{1,0:T(8,128)(2,1)}), bf16[512,256]{1,0:T(8,128)(2,1)}) %reduce-scatter.35.cloned.1.call-update) | async-done | bytes 262160 | tf_op jit(solution)/shard_map/reduce_scatter | solution.py:321
  603.8 76.1 %reduce-scatter.21.cloned.1.call-done = bf16[192,1024]{1,0:T(8,128)(2,1)} async-done(((bf16[1536,1024]{1,0:T(8,128)(2,1)}), bf16[192,1024]{1,0:T(8,128)(2,1)}) %reduce-scatter.21.cloned.1.call-update) | async-done | bytes 393232 | tf_op jit(solution)/shard_map/reduce_scatter | solution.py:289
  679.9 77.0 %reduce-scatter.17.cloned.1.call-done = bf16[192,1024]{1,0:T(8,128)(2,1)} async-done(((bf16[1536,1024]{1,0:T(8,128)(2,1)}), bf16[192,1024]{1,0:T(8,128)(2,1)}) %reduce-scatter.17.cloned.1.call-update) | async-done | bytes 393232 | tf_op jit(solution)/shard_map/reduce_scatter | solution.py:289
  758.5 75.5 %reduce-scatter.19.cloned.1.call-done = bf16[192,1024]{1,0:T(8,128)(2,1)} async-done(((bf16[1536,1024]{1,0:T(8,128)(2,1)}), bf16[192,1024]{1,0:T(8,128)(2,1)}) %reduce-scatter.19.cloned.1.call-update) | async-done | bytes 393232 | tf_op jit(solution)/shard_map/reduce_scatter | solution.py:292
  834.0 77.2 %reduce-scatter.23.cloned.1.call-done = bf16[192,1024]{1,0:T(8,128)(2,1)} async-done(((bf16[1536,1024]{1,0:T(8,128)(2,1)}), bf16[192,1024]{1,0:T(8,128)(2,1)}) %reduce-scatter.23.cloned.1.call-update) | async-done | bytes 393232 | tf_op jit(solution)/shard_map/reduce_scatter | solution.py:292
  916.1 43.2 %all-reduce.12 = (f32[1024]{0:T(1024)}, f32[1024]{0:T(1024)}, f32[1024]{0:T(1024)}, f32[1024]{0:T(1024)}) all-reduce(f32[1024]{0:T(1024)S(1)} %add.341, f32[1024]{0:T(1024)S(1)} %add.342, f32[1024]{0:T(1024)S(1)} %add.343, f32[1024]{0:T(1024)S(1)} %add.344), channel_id=1, replica_groups=mesh['seq'=4,'mp'=8] {'seq','mp'}, use_global_device_ids=true, to_apply=%region_41.42 | all-reduce | flops 4096 | bytes 32768 | tf_op jit(solution)/shard_map/psum | solution.py:325
  961.0 72.1 %reduce-scatter.15.cloned.1.call-done = f32[192,1024]{1,0:T(8,128)} async-done(((f32[1536,1024]{1,0:T(8,128)}), f32[192,1024]{1,0:T(8,128)}) %reduce-scatter.15.cloned.1.call-update) | async-done | bytes 786448 | tf_op jit(solution)/shard_map/reduce_scatter | solution.py:257
  1033.0 120.7 %reduce-scatter.13.cloned.1.call-done = f32[192,1024]{1,0:T(8,128)} async-done(((f32[1536,1024]{1,0:T(8,128)}), f32[192,1024]{1,0:T(8,128)}) %reduce-scatter.13.cloned.1.call-update) | async-done | bytes 786448 | tf_op jit(solution)/shard_map/reduce_scatter | solution.py:257
  (648 shorter events, 336.1 us)
Async XLA Ops:
  7.2 7.1 copy-start.48
  7.2 69.2 %all-gather.19.cloned.1.call-start = ((), (), s32[]{:S(2)}) async-start(), calls=%async_computation.17 | async-start | bytes 3538944 | tf_op jit(solution)/shard_map/all_gather | solution.py:240
  13.5 123.8 %all-gather.11.cloned.1.call-start = ((), (), s32[]{:S(2)}) async-start(), calls=%async_computation.12 | async-start | bytes 3538944 | tf_op jit(solution)/shard_map/all_gather | solution.py:240
  14.2 13.7 %copy-start.75 = (bf16[256,128]{1,0:T(8,128)(2,1)S(1)}, bf16[256,128]{1,0:T(8,128)(2,1)}, u32[]{:S(2)}) copy-start(bf16[256,128]{1,0:T(8,128)(2,1)} %param.28) | copy-start | bytes 196612
  14.2 207.2 %all-gather.25.cloned.1.call-start = ((), (), s32[]{:S(2)}) async-start(), calls=%async_computation.31 | async-start | bytes 3538944 | tf_op jit(solution)/shard_map/all_gather | solution.py:265
  15.3 18.5 %copy-start.95 = (s32[2,1,3]{2,1,0:T(1,128)S(1)}, s32[2,1,3]{2,1,0:T(1,128)}, u32[]{:S(2)}) copy-start(s32[2,1,3]{2,1,0:T(1,128)} %param.34) | copy-start | bytes 76
  15.3 20.4 %copy-start.76 = (bf16[256,128]{1,0:T(8,128)(2,1)S(1)}, bf16[256,128]{1,0:T(8,128)(2,1)}, u32[]{:S(2)}) copy-start(bf16[256,128]{1,0:T(8,128)(2,1)} %param.30) | copy-start | bytes 196612
  15.3 26.2 %copy-start.77 = (bf16[128,256]{1,0:T(8,128)(2,1)S(1)}, bf16[128,256]{1,0:T(8,128)(2,1)}, u32[]{:S(2)}) copy-start(bf16[128,256]{1,0:T(8,128)(2,1)} %param.31) | copy-start | bytes 196612
  15.3 359.6 %all-gather.23.cloned.1.call-start = ((), (), s32[]{:S(2)}) async-start(), calls=%async_computation.30 | async-start | bytes 3538944 | tf_op jit(solution)/shard_map/all_gather | solution.py:265
  15.9 461.9 %all-gather.15.cloned.1.call-start = ((), (), s32[]{:S(2)}) async-start(), calls=%async_computation.14 | async-start | bytes 1310720 | tf_op jit(solution)/shard_map/all_gather | solution.py:232
  16.5 461.3 %all-gather.13.cloned.1.call-start = ((), (), s32[]{:S(2)}) async-start(), calls=%async_computation.13 | async-start | bytes 3538944 | tf_op jit(solution)/shard_map/all_gather | solution.py:241
  17.1 472.9 %all-gather.21.cloned.1.call-start = ((), (), s32[]{:S(2)}) async-start(), calls=%async_computation.18 | async-start | bytes 3538944 | tf_op jit(solution)/shard_map/all_gather | solution.py:241
  17.8 484.2 %all-gather.17.cloned.1.call-start = ((), (), s32[]{:S(2)}) async-start(), calls=%async_computation.15 | async-start | bytes 1310720 | tf_op jit(solution)/shard_map/all_gather | solution.py:233
  18.6 544.8 %reduce-scatter.27.cloned.1.call-start = ((), (), s32[]{:S(2)}) async-start(), calls=%async_computation.25 | async-start | bytes 327680 | tf_op jit(solution)/shard_map/reduce_scatter | solution.py:309
  18.7 60.8 %copy-start.10 = (bf16[3,2,512,64]{2,3,1,0:T(8,128)(2,1)}, bf16[3,2,512,64]{2,3,1,0:T(8,128)(2,1)S(1)}, u32[]{:S(2)}) copy-start(bf16[3,2,512,64]{2,3,1,0:T(8,128)(2,1)S(1)} %fusion.373) | copy-start | bytes 1179652
  33.8 45.7 %copy-start.22 = (bf16[1024,128]{1,0:T(8,128)(2,1)}, bf16[1024,128]{1,0:T(8,128)(2,1)S(1)}, u32[]{:S(2)}) copy-start(bf16[1024,128]{1,0:T(8,128)(2,1)S(1)} %all_gather.45) | copy-start | bytes 786436
  41.5 285.3 %copy-start.18 = (bf16[1024,128]{1,0:T(8,128)(2,1)}, bf16[1024,128]{1,0:T(8,128)(2,1)S(1)}, u32[]{:S(2)}) copy-start(bf16[1024,128]{1,0:T(8,128)(2,1)S(1)} %all_gather.44) | copy-start | bytes 786436
  80.3 60.1 %copy-start = (bf16[1536,1024]{1,0:T(8,128)(2,1)S(1)}, bf16[1536,1024]{1,0:T(8,128)(2,1)}, u32[]{:S(2)}) copy-start(bf16[1536,1024]{1,0:T(8,128)(2,1)} %all-gather.19.cloned.1.call-done) | copy-start | bytes 9437188
  228.1 80.7 %copy-start.51 = (f32[64,64,1]{1,0,2:T(8,128)S(1)}, f32[64,64,1]{1,0,2:T(8,128)}, u32[]{:S(2)}) copy-start(f32[64,64,1]{1,0,2:T(8,128)} %constant.421) | copy-start | bytes 49156
  228.2 80.7 %copy-start.94 = (f32[64]{0:T(128)S(1)}, f32[64]{0:T(128)}, u32[]{:S(2)}) copy-start(f32[64]{0:T(128)} %constant.420) | copy-start | bytes 772
  316.6 10.2 copy-start.3
  332.6 42.4 %copy-start.20 = (bf16[128,1024]{1,0:T(8,128)(2,1)S(1)}, bf16[128,1024]{1,0:T(8,128)(2,1)}, u32[]{:S(2)}) copy-start(bf16[128,1024]{1,0:T(8,128)(2,1)} %all_gather.46) | copy-start | bytes 786436
  456.3 19.9 %copy-start.33 = (bf16[3,2,8,8,512]{4,3,0,2,1:T(8,128)(2,1)}, bf16[3,2,8,8,512]{4,3,0,2,1:T(8,128)(2,1)S(1)}, u32[]{:S(2)}) copy-start(bf16[3,2,8,8,512]{4,3,0,2,1:T(8,128)(2,1)S(1)} %copy.187) | copy-start | bytes 1179652
  461.0 104.0 %reduce-scatter.25.cloned.1.call-start = ((), (), s32[]{:S(2)}) async-start(), calls=%async_computation.24 | async-start | bytes 327680 | tf_op jit(solution)/shard_map/reduce_scatter | solution.py:306
  468.6 97.9 %reduce-scatter.29.cloned.1.call-start = ((), (), s32[]{:S(2)}) async-start(), calls=%async_computation.26 | async-start | bytes 327680 | tf_op jit(solution)/shard_map/reduce_scatter | solution.py:312
  473.4 94.6 %reduce-scatter.31.cloned.1.call-start = ((), (), s32[]{:S(2)}) async-start(), calls=%async_computation.27 | async-start | bytes 327680 | tf_op jit(solution)/shard_map/reduce_scatter | solution.py:315
  477.7 97.1 %reduce-scatter.33.cloned.1.call-start = ((), (), s32[]{:S(2)}) async-start(), calls=%async_computation.28 | async-start | bytes 1310720 | tf_op jit(solution)/shard_map/reduce_scatter | solution.py:318
  502.0 6.2 copy-start.96
  519.8 82.3 %reduce-scatter.35.cloned.1.call-start = ((), (), s32[]{:S(2)}) async-start(), calls=%async_computation.29 | async-start | bytes 1310720 | tf_op jit(solution)/shard_map/reduce_scatter | solution.py:321
  527.0 152.9 %reduce-scatter.21.cloned.1.call-start = ((), (), s32[]{:S(2)}) async-start(), calls=%async_computation.22 | async-start | bytes 3538944 | tf_op jit(solution)/shard_map/reduce_scatter | solution.py:289
  533.1 223.8 %reduce-scatter.17.cloned.1.call-start = ((), (), s32[]{:S(2)}) async-start(), calls=%async_computation.20 | async-start | bytes 3538944 | tf_op jit(solution)/shard_map/reduce_scatter | solution.py:289
  538.8 295.2 %reduce-scatter.19.cloned.1.call-start = ((), (), s32[]{:S(2)}) async-start(), calls=%async_computation.21 | async-start | bytes 3538944 | tf_op jit(solution)/shard_map/reduce_scatter | solution.py:292
  544.0 367.3 %reduce-scatter.23.cloned.1.call-start = ((), (), s32[]{:S(2)}) async-start(), calls=%async_computation.23 | async-start | bytes 3538944 | tf_op jit(solution)/shard_map/reduce_scatter | solution.py:292
  549.0 484.1 %reduce-scatter.15.cloned.1.call-start = ((), (), s32[]{:S(2)}) async-start(), calls=%async_computation.19 | async-start | bytes 7077888 | tf_op jit(solution)/shard_map/reduce_scatter | solution.py:257
  556.2 597.6 %reduce-scatter.13.cloned.1.call-start = ((), (), s32[]{:S(2)}) async-start(), calls=%async_computation.16 | async-start | bytes 7077888 | tf_op jit(solution)/shard_map/reduce_scatter | solution.py:257
  563.3 193.6 %copy-start.7 = (bf16[2,192,1024]{2,1,0:T(8,128)(2,1)S(1)}, bf16[2,192,1024]{2,1,0:T(8,128)(2,1)}, u32[]{:S(2)}) copy-start(bf16[2,192,1024]{2,1,0:T(8,128)(2,1)} %param.23) | copy-start | bytes 2359300
  563.3 193.6 %copy-start.73 = (f32[1024]{0:T(1024)S(1)}, f32[1024]{0:T(1024)}, u32[]{:S(2)}) copy-start(f32[1024]{0:T(1024)} %param.24) | copy-start | bytes 12292
  563.3 193.6 %copy-start.79 = (f32[192]{0:T(256)S(1)}, f32[192]{0:T(256)}, u32[]{:S(2)}) copy-start(f32[192]{0:T(256)} %copy-done.78) | copy-start | bytes 2308
  563.3 193.6 %copy-start.81 = (f32[192]{0:T(256)S(1)}, f32[192]{0:T(256)}, u32[]{:S(2)}) copy-start(f32[192]{0:T(256)} %copy-done.80) | copy-start | bytes 2308
  563.3 195.1 %copy-start.92 = (f32[192]{0:T(256)S(1)}, f32[192]{0:T(256)}, u32[]{:S(2)}) copy-start(f32[192]{0:T(256)} %copy-done.91) | copy-start | bytes 2308
  563.4 195.1 %copy-start.90 = (f32[192]{0:T(256)S(1)}, f32[192]{0:T(256)}, u32[]{:S(2)}) copy-start(f32[192]{0:T(256)} %copy-done.89) | copy-start | bytes 2308
  563.4 347.9 %copy-start.72 = (f32[1024]{0:T(1024)S(1)}, f32[1024]{0:T(1024)}, u32[]{:S(2)}) copy-start(f32[1024]{0:T(1024)} %param.26) | copy-start | bytes 12292
  563.4 347.9 %copy-start.83 = (f32[192]{0:T(256)S(1)}, f32[192]{0:T(256)}, u32[]{:S(2)}) copy-start(f32[192]{0:T(256)} %copy-done.82) | copy-start | bytes 2308
  563.4 347.9 %copy-start.88 = (f32[192]{0:T(256)S(1)}, f32[192]{0:T(256)}, u32[]{:S(2)}) copy-start(f32[192]{0:T(256)} %copy-done.87) | copy-start | bytes 2308
  679.9 279.5 %copy-start.36 = (bf16[192,1024]{1,0:T(8,128)(2,1)S(1)}, bf16[192,1024]{1,0:T(8,128)(2,1)}, u32[]{:S(2)}) copy-start(bf16[192,1024]{1,0:T(8,128)(2,1)} %reduce-scatter.21.cloned.1.call-done) | copy-start | bytes 1179652
  911.2 48.2 %copy-start.38 = (bf16[192,1024]{1,0:T(8,128)(2,1)S(1)}, bf16[192,1024]{1,0:T(8,128)(2,1)}, u32[]{:S(2)}) copy-start(bf16[192,1024]{1,0:T(8,128)(2,1)} %reduce-scatter.23.cloned.1.call-done) | copy-start | bytes 1179652
  911.3 242.5 %copy-start.39 = (bf16[192,1024]{1,0:T(8,128)(2,1)S(1)}, bf16[192,1024]{1,0:T(8,128)(2,1)}, u32[]{:S(2)}) copy-start(bf16[192,1024]{1,0:T(8,128)(2,1)} %reduce-scatter.17.cloned.1.call-done) | copy-start | bytes 1179652
  911.3 242.5 %copy-start.40 = (bf16[192,1024]{1,0:T(8,128)(2,1)S(1)}, bf16[192,1024]{1,0:T(8,128)(2,1)}, u32[]{:S(2)}) copy-start(bf16[192,1024]{1,0:T(8,128)(2,1)} %reduce-scatter.19.cloned.1.call-done) | copy-start | bytes 1179652
  (83 other events, 248.7 us)
Sparse Core Ops, SparseCore 0:
  13.6 62.7 all-gather.18
  78.5 58.6 all-gather.10
  139.4 58.6 all-gather.24
  200.2 58.6 all-gather.22
  260.3 15.3 all-gather.14
  277.8 60.0 all-gather.12
  340.1 58.7 all-gather.20
  400.4 15.5 all-gather.16
  461.1 18.9 reduce-scatter.26
  482.4 20.0 reduce-scatter.24
  505.0 20.0 reduce-scatter.28
  527.4 20.0 reduce-scatter.30
  550.0 24.7 reduce-scatter.32
  577.2 24.7 reduce-scatter.34
  605.5 74.3 reduce-scatter.20
  683.3 73.4 reduce-scatter.16
  760.3 73.6 reduce-scatter.18
  837.5 73.7 reduce-scatter.22
  914.8 118.1 reduce-scatter.14
  1036.5 117.2 reduce-scatter.12
where the time goes:
time: 1180 us; the launch traced here: 1170 us
  waiting for transfers between devices  617 us (52%)
  matrix products  282 us (24%)
  local copies, waits for them, and re-layouts  104 us (9%)
  blocking collectives  68.9 us (6%)
  other arithmetic  58.9 us (5%)
  loops' own time  17.9 us (2%)
  between operations  16.3 us (1%)
    reduce_scatter x2, waiting for transfers between devices, local(): lax.psum_scatter(jnp.dot(context_rows, w_out, preferred_element_type=jnp....  193 us
    reduce_scatter x2, waiting for transfers between devices, local(): lax.psum_scatter(part_one.astype(jnp.bfloat16), 'mp', scatter_dimension=0...  153 us
    reduce_scatter x2, waiting for transfers between devices, local(): lax.psum_scatter(part_two.astype(jnp.bfloat16), 'mp', scatter_dimension=0...  153 us
    all_gather x2, waiting for transfers between devices, local(): lax.all_gather(normed_one.astype(jnp.bfloat16), 'mp', axis=0, tiled=True)  83.5 us
    dot_general x24, matrix products, block_step(): jnp.einsum('ugy,uky->ugk', block_of_queries, block_of_keys, precision=max...  55 us
    dot_general x24, matrix products, block_step(): jnp.einsum('hqk,hkd->hqd', attention_scores, value_block, precision=maxim...  54.8 us
    psum x1, blocking collectives, local(): lax.psum((norm_sums[0], norm_sums[1], norm_sums[2], norm_sums[3]), ('seq'...  43.2 us
    dot_general x12, matrix products, contract_cols(): lax.dot_general(left_side, right_side, (((1,), (1,)), ((), ())), preferre...  32.5 us
  transfers between devices with their start and end apart: 20, of which 10 were waited for; matrix products, arithmetic and copies ran while one was open for 36% of the time, Pallas kernels for 0%

commit v1 on v0

--- a/solution.py
+++ b/solution.py
@@ -8,6 +8,18 @@
 HEAD_DIM = 64
 ROT = 16
 FEATS = 64
+
+
+def collect(x, axis, dim):
+    ways, here = (lax.axis_size(axis), lax.axis_index(axis))
+    grown, reach = (x, 1)
+    while reach < ways:
+        theirs = lax.ppermute(grown, axis, [(d, d ^ reach) for d in range(ways)])
+        mine_first = jnp.concatenate([grown, theirs], axis=dim)
+        theirs_first = jnp.concatenate([theirs, grown], axis=dim)
+        grown = jnp.where(here & reach == 0, mine_first, theirs_first)
+        reach = 2 * reach
+    return grown
 
 
 def prime_list(wanted):
@@ -237,7 +249,7 @@
         normed_one, pull_one = jax.vjp(layer_norm, rows_in, ln1_gain, ln1_bias)
         normed_two, pull_two = jax.vjp(layer_norm, rows_in, ln2_gain, ln2_bias)
         group_one, group_two = (
-            lax.all_gather(normed_one.astype(jnp.bfloat16), "mp", axis=0, tiled=True),
+            collect(normed_one.astype(jnp.bfloat16), "mp", 0),
             lax.all_gather(normed_two.astype(jnp.bfloat16), "mp", axis=0, tiled=True),
         )
         plain_query_rows = jnp.dot(group_one, w_query, preferred_element_type=jnp.float32)

time: 1180 us -> 1340 us (1.14)
  waiting for transfers between devices: 617 us -> 732 us
  local copies, waits for them, and re-layouts: 104 us -> 122 us
  other arithmetic: 58.9 us -> 73.6 us
    ppermute x0 -> x6, waiting for transfers between devices: none -> 192 us  [collect(): theirs = lax.ppermute(grown, axis, [(d, d ^ reach) for d in range(ways)])]
    all_gather x2 -> x0, waiting for transfers between devices: 83.5 us -> none  [local(): lax.all_gather(normed_one.astype(jnp.bfloat16), 'mp', axis=0, tiled=True)]
    unnamed x226 -> x243, local copies, waits for them, and re-layouts: 30.4 us -> 24 us
  transfers between devices with their start and end apart: 20 -> 24, of which waited for: 10 -> 13; matrix products, arithmetic and copies ran while one was open for 36% -> 35% of each run, Pallas kernels for 0% -> 0%
where the time goes in v1:
time: 1340 us; the launch traced here: 1330 us
  waiting for transfers between devices  732 us (55%)
  matrix products  292 us (22%)
  local copies, waits for them, and re-layouts  122 us (9%)
  other arithmetic  73.6 us (5%)
  blocking collectives  68 us (5%)
  loops' own time  18.1 us (1%)
  between operations  16.2 us (1%)
    reduce_scatter x2, waiting for transfers between devices, local(): lax.psum_scatter(jnp.dot(context_rows, w_out, preferred_element_type=jnp....  193 us
    ppermute x6, waiting for transfers between devices, collect(): theirs = lax.ppermute(grown, axis, [(d, d ^ reach) for d in range(ways)])  192 us
    reduce_scatter x2, waiting for transfers between devices, local(): lax.psum_scatter(part_one.astype(jnp.bfloat16), 'mp', scatter_dimension=0...  154 us
    reduce_scatter x2, waiting for transfers between devices, local(): lax.psum_scatter(part_two.astype(jnp.bfloat16), 'mp', scatter_dimension=0...  153 us
    dot_general x24, matrix products, block_step(): jnp.einsum('hqk,hkd->hqd', attention_scores, value_block, precision=maxim...  58.7 us
    dot_general x24, matrix products, block_step(): jnp.einsum('ugy,uky->ugk', block_of_queries, block_of_keys, precision=max...  58 us
    psum x1, blocking collectives, local(): lax.psum((norm_sums[0], norm_sums[1], norm_sums[2], norm_sums[3]), ('seq'...  43.4 us
    dot_general x12, matrix products, contract_cols(): lax.dot_general(left_side, right_side, (((1,), (1,)), ((), ())), preferre...  33.4 us
  transfers between devices with their start and end apart: 24, of which 13 were waited for; matrix products, arithmetic and copies ran while one was open for 35% of the time, Pallas kernels for 0%

profile of v1, /device:TPU:0, one launch (start us, length us, event | category | flops | bytes accessed | tf_op | source)
XLA Modules:
  0.0 1329.5 jit_solution(10760383643183163629)
XLA Ops:
  14.2 3.1 collective-permute-start.3
  17.8 13.2 collective-permute-done.3
  33.9 5.8 all_gather.36
  41.2 45.7 %collective-permute-done.4 = bf16[384,1024]{1,0:T(8,128)(2,1)S(1)} collective-permute-done((bf16[384,1024]{1,0:T(8,128)(2,1)S(1)}, bf16[384,1024]{1,0:T(8,128)(2,1)S(1)}, u32[]{:S(2)}, u32[]{:S(2)}) %collective-permute-start.4) | collective-permute-done | bytes 786464 | tf_op jit(solution)/shard_map/ppermute | solution.py:17
  87.7 7.2 all_gather.38
  95.0 5.8 all_gather.37
  101.0 16.1 %collective-permute-done.1 = bf16[384,1024]{1,0:T(8,128)(2,1)S(1)} collective-permute-done((bf16[384,1024]{1,0:T(8,128)(2,1)S(1)}, bf16[384,1024]{1,0:T(8,128)(2,1)S(1)}, u32[]{:S(2)}, u32[]{:S(2)}) %collective-permute-start.1) | collective-permute-done | bytes 786464 | tf_op jit(solution)/shard_map/ppermute | solution.py:17
  119.0 5.8 all_gather.39
  129.3 102.2 %collective-permute-done.5 = bf16[768,1024]{1,0:T(8,128)(2,1)} collective-permute-done((bf16[768,1024]{1,0:T(8,128)(2,1)S(1)}, bf16[768,1024]{1,0:T(8,128)(2,1)}, u32[]{:S(2)}, u32[]{:S(2)}) %collective-permute-start.5) | collective-permute-done | bytes 1572896 | tf_op jit(solution)/shard_map/ppermute | solution.py:17
  236.8 14.8 %collective-permute-done.2 = bf16[768,1024]{1,0:T(8,128)(2,1)} collective-permute-done((bf16[768,1024]{1,0:T(8,128)(2,1)}, bf16[768,1024]{1,0:T(8,128)(2,1)}, u32[]{:S(2)}, u32[]{:S(2)}) %collective-permute-start.2) | collective-permute-done | bytes 1572896 | tf_op jit(solution)/shard_map/ppermute | solution.py:17
  251.7 3.5 maximum_select_fusion
  282.1 54.4 %while.95 = (s32[]{:T(128)}, f32[2,64,64]{2,1,0:T(8,128)S(1)}, f32[2,64]{1,0:T(2,128)S(1)}, s32[]{:T(128)}, bf16[3,2,512,64]{2,3,1,0:T(8,128)(2,1)}, /*index=5*/...) while((s32[]{:T(128)}, f32[2,64,64]{2,1,0:T(8,128)S(1)}, ...), condition=%wide.region_17.18_spmd.clone, body=%wide.region_15.17_spmd.clone.sunk | while | flops 910208896 | bytes 8144617 | solution.py:188
  291.6 3.3 fusion.628
  309.6 3.3 fusion.628
  327.6 3.3 fusion.628
  349.5 50.9 %while.94 = (s32[]{:T(128)}, f32[2,64,64]{2,1,0:T(8,128)S(1)}, f32[2,64]{1,0:T(2,128)S(1)}, s32[]{:T(128)}, bf16[3,2,512,64]{2,3,1,0:T(8,128)(2,1)}, /*index=5*/...) while((s32[]{:T(128)}, f32[2,64,64]{2,1,0:T(8,128)S(1)}, ...), condition=%wide.region_8.9_spmd.clone, body=%wide.region_6.8_spmd.clone.sunk | while | flops 910208896 | bytes 8145129 | solution.py:188
  356.6 3.3 fusion.613
  368.2 3.0 select_reduce_fusion.10
  373.6 3.3 fusion.613
  390.6 3.3 fusion.613
  404.3 3.1 fusion.240
  410.0 76.8 %while.97 = (s32[]{:T(128)}, f32[2,64,64]{2,1,0:T(8,128)S(1)}, f32[2,64]{1,0:T(2,128)S(1)}, f32[3,2,512,64]{2,3,1,0:T(8,128)}, f32[3,2,512,64]{2,3,1,0:T(8,128)}...) while((s32[]{:T(128)}, f32[2,64,64]{2,1,0:T(8,128)S(1)}, ...), condition=%wide.region_32.33_spmd.clone, body=%wide.region_29.32_spmd.clone.sunk | while | flops 2675472384 | bytes 24581376 | solution.py:188
  471.0 3.0 fusion.698
  494.7 3.9 fusion.248
  503.0 102.0 %while.96 = (s32[]{:T(128)}, f32[2,64,64]{2,1,0:T(8,128)}, f32[2,64]{1,0:T(2,128)}, f32[3,2,512,64]{2,3,1,0:T(8,128)}, f32[3,2,512,64]{2,3,1,0:T(8,128)}, /*inde...) while((s32[]{:T(128)}, f32[2,64,64]{2,1,0:T(8,128)}, ...), condition=%wide.region_22.23_spmd.clone, body=%wide.region_19.22_spmd.clone.sunk | while | flops 2675472384 | bytes 27727188 | solution.py:188
  515.1 3.0 select_reduce_fusion.12
  518.4 3.0 fusion.663
  549.6 3.0 select_reduce_fusion.12
  552.9 3.0 fusion.663
  584.0 3.0 select_reduce_fusion.12
  587.4 3.0 fusion.663
  634.2 12.0 multiply_convert_fusion.1
  646.2 12.1 multiply_convert_fusion
  658.4 6.2 add_convert_fusion.3
  676.1 4.3 fusion.234
  696.8 3.5 convolution_convert_fusion.1
  701.6 3.6 convolution_convert_fusion
  708.8 3.6 convolution_add_fusion.8
  715.8 3.7 convolution_add_fusion.9
  725.8 12.5 reduce-scatter.33.cloned.1.call-done
  740.1 25.4 %reduce-scatter.35.cloned.1.call-done = bf16[512,256]{1,0:T(8,128)(2,1)} async-done(((bf16[512,1024]{1,0:T(8,128)(2,1)}), bf16[512,256]{1,0:T(8,128)(2,1)}) %reduce-scatter.35.cloned.1.call-update) | async-done | bytes 262160 | tf_op jit(solution)/shard_map/reduce_scatter | solution.py:333
  767.3 76.5 %reduce-scatter.21.cloned.1.call-done = bf16[192,1024]{1,0:T(8,128)(2,1)} async-done(((bf16[1536,1024]{1,0:T(8,128)(2,1)}), bf16[192,1024]{1,0:T(8,128)(2,1)}) %reduce-scatter.21.cloned.1.call-update) | async-done | bytes 393232 | tf_op jit(solution)/shard_map/reduce_scatter | solution.py:301
  843.8 77.2 %reduce-scatter.17.cloned.1.call-done = bf16[192,1024]{1,0:T(8,128)(2,1)} async-done(((bf16[1536,1024]{1,0:T(8,128)(2,1)}), bf16[192,1024]{1,0:T(8,128)(2,1)}) %reduce-scatter.17.cloned.1.call-update) | async-done | bytes 393232 | tf_op jit(solution)/shard_map/reduce_scatter | solution.py:301
  922.7 75.7 %reduce-scatter.19.cloned.1.call-done = bf16[192,1024]{1,0:T(8,128)(2,1)} async-done(((bf16[1536,1024]{1,0:T(8,128)(2,1)}), bf16[192,1024]{1,0:T(8,128)(2,1)}) %reduce-scatter.19.cloned.1.call-update) | async-done | bytes 393232 | tf_op jit(solution)/shard_map/reduce_scatter | solution.py:304
  998.4 77.3 %reduce-scatter.23.cloned.1.call-done = bf16[192,1024]{1,0:T(8,128)(2,1)} async-done(((bf16[1536,1024]{1,0:T(8,128)(2,1)}), bf16[192,1024]{1,0:T(8,128)(2,1)}) %reduce-scatter.23.cloned.1.call-update) | async-done | bytes 393232 | tf_op jit(solution)/shard_map/reduce_scatter | solution.py:304
  1080.5 43.4 %all-reduce.12 = (f32[1024]{0:T(1024)}, f32[1024]{0:T(1024)}, f32[1024]{0:T(1024)}, f32[1024]{0:T(1024)}) all-reduce(f32[1024]{0:T(1024)S(1)} %add.341, f32[1024]{0:T(1024)S(1)} %add.342, f32[1024]{0:T(1024)S(1)} %add.343, f32[1024]{0:T(1024)S(1)} %add.344), channel_id=1, replica_groups=mesh['seq'=4,'mp'=8] {'seq','mp'}, use_global_device_ids=true, to_apply=%region_41.42 | all-reduce | flops 4096 | bytes 32768 | tf_op jit(solution)/shard_map/psum | solution.py:337
  1125.5 71.8 %reduce-scatter.15.cloned.1.call-done = f32[192,1024]{1,0:T(8,128)} async-done(((f32[1536,1024]{1,0:T(8,128)}), f32[192,1024]{1,0:T(8,128)}) %reduce-scatter.15.cloned.1.call-update) | async-done | bytes 786448 | tf_op jit(solution)/shard_map/reduce_scatter | solution.py:269
  1197.3 120.8 %reduce-scatter.13.cloned.1.call-done = f32[192,1024]{1,0:T(8,128)} async-done(((f32[1536,1024]{1,0:T(8,128)}), f32[192,1024]{1,0:T(8,128)}) %reduce-scatter.13.cloned.1.call-update) | async-done | bytes 786448 | tf_op jit(solution)/shard_map/reduce_scatter | solution.py:269
  (695 shorter events, 391.6 us)
Async XLA Ops:
  7.2 397.1 %all-gather.19.cloned.1.call-start = ((), (), s32[]{:S(2)}) async-start(), calls=%async_computation.29 | async-start | bytes 3538944 | tf_op jit(solution)/shard_map/all_gather | solution.py:277
  9.4 485.2 %all-gather.17.cloned.1.call-start = ((), (), s32[]{:S(2)}) async-start(), calls=%async_computation.28 | async-start | bytes 3538944 | tf_op jit(solution)/shard_map/all_gather | solution.py:277
  10.2 624.0 %all-gather.11.cloned.1.call-start = ((), (), s32[]{:S(2)}) async-start(), calls=%async_computation.13 | async-start | bytes 1310720 | tf_op jit(solution)/shard_map/all_gather | solution.py:244
  10.9 623.3 %all-gather.9.cloned.1.call-start = ((), (), s32[]{:S(2)}) async-start(), calls=%async_computation.12 | async-start | bytes 3538944 | tf_op jit(solution)/shard_map/all_gather | solution.py:253
  13.6 632.6 %all-gather.15.cloned.1.call-start = ((), (), s32[]{:S(2)}) async-start(), calls=%async_computation.16 | async-start | bytes 3538944 | tf_op jit(solution)/shard_map/all_gather | solution.py:253
  14.1 644.2 %all-gather.13.cloned.1.call-start = ((), (), s32[]{:S(2)}) async-start(), calls=%async_computation.14 | async-start | bytes 1310720 | tf_op jit(solution)/shard_map/all_gather | solution.py:245
  14.2 16.8 %collective-permute-start.3 = (bf16[192,1024]{1,0:T(8,128)(2,1)S(1)}, bf16[192,1024]{1,0:T(8,128)(2,1)S(1)}, u32[]{:S(2)}, u32[]{:S(2)}) collective-permute-start(bf16[192,1024]{1,0:T(8,128)(2,1)S(1)} %get-tuple-element.1358), channel_id=1, source_target_pairs={{0,1},{1,0},{2,3},{3,2},{4,5},{5,4},{6,7},{7,6},{8,9},{9,8},{10,11... | collective-permute-start | bytes 1179656 | tf_op jit(solution)/shard_map/ppermute | solution.py:17
  17.3 22.5 %collective-permute-start = (bf16[192,1024]{1,0:T(8,128)(2,1)S(1)}, bf16[192,1024]{1,0:T(8,128)(2,1)S(1)}, u32[]{:S(2)}, u32[]{:S(2)}) collective-permute-start(bf16[192,1024]{1,0:T(8,128)(2,1)S(1)} %get-tuple-element.1359), channel_id=1, source_target_pairs={{0,1},{1,0},{2,3},{3,2},{4,5},{5,4},{6,7},{7,6},{8,9},{9,8},{10,11... | collective-permute-start | bytes 1179656 | tf_op jit(solution)/shard_map/ppermute | solution.py:17
  17.4 702.3 %reduce-scatter.29.cloned.1.call-start = ((), (), s32[]{:S(2)}) async-start(), calls=%async_computation.24 | async-start | bytes 327680 | tf_op jit(solution)/shard_map/reduce_scatter | solution.py:324
  17.8 69.9 %copy-start.84 = (bf16[256,128]{1,0:T(8,128)(2,1)S(1)}, bf16[256,128]{1,0:T(8,128)(2,1)}, u32[]{:S(2)}) copy-start(bf16[256,128]{1,0:T(8,128)(2,1)} %param.28) | copy-start | bytes 196612
  17.8 77.2 %copy-start.85 = (bf16[256,128]{1,0:T(8,128)(2,1)S(1)}, bf16[256,128]{1,0:T(8,128)(2,1)}, u32[]{:S(2)}) copy-start(bf16[256,128]{1,0:T(8,128)(2,1)} %param.30) | copy-start | bytes 196612
  31.3 55.7 %collective-permute-start.4 = (bf16[384,1024]{1,0:T(8,128)(2,1)S(1)}, bf16[384,1024]{1,0:T(8,128)(2,1)S(1)}, u32[]{:S(2)}, u32[]{:S(2)}) collective-permute-start(bf16[384,1024]{1,0:T(8,128)(2,1)S(1)} %maximum_select_fusion.5), channel_id=1, source_target_pairs={{0,2},{1,3},{2,0},{3,1},{4,6},{5,7},{6,4},{7,5},{8,10},{9,11},{10,... | collective-permute-start | bytes 2359304 | tf_op jit(solution)/shard_map/ppermute | solution.py:17
  39.7 217.6 %copy-start.25 = (bf16[1024,128]{1,0:T(8,128)(2,1)}, bf16[1024,128]{1,0:T(8,128)(2,1)S(1)}, u32[]{:S(2)}) copy-start(bf16[1024,128]{1,0:T(8,128)(2,1)S(1)} %all_gather.36) | copy-start | bytes 786436
  40.1 78.9 %copy-start.86 = (bf16[128,256]{1,0:T(8,128)(2,1)S(1)}, bf16[128,256]{1,0:T(8,128)(2,1)}, u32[]{:S(2)}) copy-start(bf16[128,256]{1,0:T(8,128)(2,1)} %param.31) | copy-start | bytes 196612
  40.1 77.0 %collective-permute-start.1 = (bf16[384,1024]{1,0:T(8,128)(2,1)S(1)}, bf16[384,1024]{1,0:T(8,128)(2,1)S(1)}, u32[]{:S(2)}, u32[]{:S(2)}) collective-permute-start(bf16[384,1024]{1,0:T(8,128)(2,1)S(1)} %maximum_select_fusion.4), channel_id=1, source_target_pairs={{0,2},{1,3},{2,0},{3,1},{4,6},{5,7},{6,4},{7,5},{8,10},{9,11},{10,... | collective-permute-start | bytes 2359304 | tf_op jit(solution)/shard_map/ppermute | solution.py:17
  87.6 143.8 %collective-permute-start.5 = (bf16[768,1024]{1,0:T(8,128)(2,1)S(1)}, bf16[768,1024]{1,0:T(8,128)(2,1)}, u32[]{:S(2)}, u32[]{:S(2)}) collective-permute-start(bf16[768,1024]{1,0:T(8,128)(2,1)S(1)} %maximum_select_fusion.3), channel_id=1, source_target_pairs={{0,4},{1,5},{2,6},{3,7},{4,0},{5,1},{6,2},{7,3},{8,12},{9,13},{10,... | collective-permute-start | bytes 4718600 | tf_op jit(solution)/shard_map/ppermute | solution.py:17
  95.0 160.2 %copy-start.27 = (bf16[1024,128]{1,0:T(8,128)(2,1)}, bf16[1024,128]{1,0:T(8,128)(2,1)S(1)}, u32[]{:S(2)}) copy-start(bf16[1024,128]{1,0:T(8,128)(2,1)S(1)} %all_gather.38) | copy-start | bytes 786436
  100.8 160.6 %copy-start.21 = (bf16[1024,128]{1,0:T(8,128)(2,1)}, bf16[1024,128]{1,0:T(8,128)(2,1)S(1)}, u32[]{:S(2)}) copy-start(bf16[1024,128]{1,0:T(8,128)(2,1)S(1)} %all_gather.37) | copy-start | bytes 786436
  100.9 133.5 %copy-start.14 = (bf16[3,2,512,64]{2,3,1,0:T(8,128)(2,1)}, bf16[3,2,512,64]{2,3,1,0:T(8,128)(2,1)S(1)}, u32[]{:S(2)}) copy-start(bf16[3,2,512,64]{2,3,1,0:T(8,128)(2,1)S(1)} %fusion.373) | copy-start | bytes 1179652
  118.9 132.7 %collective-permute-start.2 = (bf16[768,1024]{1,0:T(8,128)(2,1)}, bf16[768,1024]{1,0:T(8,128)(2,1)}, u32[]{:S(2)}, u32[]{:S(2)}) collective-permute-start(bf16[768,1024]{1,0:T(8,128)(2,1)} %maximum_select_fusion.2), channel_id=1, source_target_pairs={{0,4},{1,5},{2,6},{3,7},{4,0},{5,1},{6,2},{7,3},{8,12},{9,13},{10,... | collective-permute-start | bytes 4718600 | tf_op jit(solution)/shard_map/ppermute | solution.py:17
  124.7 369.9 %copy-start.23 = (bf16[128,1024]{1,0:T(8,128)(2,1)}, bf16[128,1024]{1,0:T(8,128)(2,1)S(1)}, u32[]{:S(2)}) copy-start(bf16[128,1024]{1,0:T(8,128)(2,1)S(1)} %all_gather.39) | copy-start | bytes 786436
  129.3 135.1 %copy-start.67 = (f32[1536,8]{0,1:T(8,128)}, f32[1536,8]{0,1:T(8,128)S(1)}, u32[]{:S(2)}) copy-start(f32[1536,8]{0,1:T(8,128)S(1)} %get-tuple-element.1387) | copy-start | bytes 147460
  129.3 135.1 %copy-start.69 = (f32[1536,8]{0,1:T(8,128)}, f32[1536,8]{0,1:T(8,128)S(1)}, u32[]{:S(2)}) copy-start(f32[1536,8]{0,1:T(8,128)S(1)} %get-tuple-element.1388) | copy-start | bytes 147460
  409.9 78.1 %copy-start.20 = (f32[2,1536,64]{1,2,0:T(8,128)S(1)}, f32[2,1536,64]{1,2,0:T(8,128)}, u32[]{:S(2)}) copy-start(f32[2,1536,64]{1,2,0:T(8,128)} %copy-done.19) | copy-start | bytes 2359300
  409.9 78.1 %copy-start.102 = (f32[64]{0:T(128)S(1)}, f32[64]{0:T(128)}, u32[]{:S(2)}) copy-start(f32[64]{0:T(128)} %constant.430) | copy-start | bytes 772
  620.3 100.9 %reduce-scatter.27.cloned.1.call-start = ((), (), s32[]{:S(2)}) async-start(), calls=%async_computation.23 | async-start | bytes 327680 | tf_op jit(solution)/shard_map/reduce_scatter | solution.py:321
  625.1 97.7 %reduce-scatter.25.cloned.1.call-start = ((), (), s32[]{:S(2)}) async-start(), calls=%async_computation.22 | async-start | bytes 327680 | tf_op jit(solution)/shard_map/reduce_scatter | solution.py:318
  629.8 94.5 %reduce-scatter.31.cloned.1.call-start = ((), (), s32[]{:S(2)}) async-start(), calls=%async_computation.25 | async-start | bytes 327680 | tf_op jit(solution)/shard_map/reduce_scatter | solution.py:327
  634.1 104.2 %reduce-scatter.33.cloned.1.call-start = ((), (), s32[]{:S(2)}) async-start(), calls=%async_computation.26 | async-start | bytes 1310720 | tf_op jit(solution)/shard_map/reduce_scatter | solution.py:330
  676.1 89.4 %reduce-scatter.35.cloned.1.call-start = ((), (), s32[]{:S(2)}) async-start(), calls=%async_computation.27 | async-start | bytes 1310720 | tf_op jit(solution)/shard_map/reduce_scatter | solution.py:333
  683.3 160.5 %reduce-scatter.21.cloned.1.call-start = ((), (), s32[]{:S(2)}) async-start(), calls=%async_computation.20 | async-start | bytes 3538944 | tf_op jit(solution)/shard_map/reduce_scatter | solution.py:301
  689.3 231.8 %reduce-scatter.17.cloned.1.call-start = ((), (), s32[]{:S(2)}) async-start(), calls=%async_computation.18 | async-start | bytes 3538944 | tf_op jit(solution)/shard_map/reduce_scatter | solution.py:301
  695.0 303.4 %reduce-scatter.19.cloned.1.call-start = ((), (), s32[]{:S(2)}) async-start(), calls=%async_computation.19 | async-start | bytes 3538944 | tf_op jit(solution)/shard_map/reduce_scatter | solution.py:304
  700.2 375.4 %reduce-scatter.23.cloned.1.call-start = ((), (), s32[]{:S(2)}) async-start(), calls=%async_computation.21 | async-start | bytes 3538944 | tf_op jit(solution)/shard_map/reduce_scatter | solution.py:304
  705.2 492.0 %reduce-scatter.15.cloned.1.call-start = ((), (), s32[]{:S(2)}) async-start(), calls=%async_computation.17 | async-start | bytes 7077888 | tf_op jit(solution)/shard_map/reduce_scatter | solution.py:269
  712.5 605.5 %reduce-scatter.13.cloned.1.call-start = ((), (), s32[]{:S(2)}) async-start(), calls=%async_computation.15 | async-start | bytes 7077888 | tf_op jit(solution)/shard_map/reduce_scatter | solution.py:269
  719.5 201.5 %copy-start.11 = (bf16[2,192,1024]{2,1,0:T(8,128)(2,1)S(1)}, bf16[2,192,1024]{2,1,0:T(8,128)(2,1)}, u32[]{:S(2)}) copy-start(bf16[2,192,1024]{2,1,0:T(8,128)(2,1)} %param.23) | copy-start | bytes 2359300
  719.5 201.5 %copy-start.82 = (f32[1024]{0:T(1024)S(1)}, f32[1024]{0:T(1024)}, u32[]{:S(2)}) copy-start(f32[1024]{0:T(1024)} %param.24) | copy-start | bytes 12292
  719.5 201.5 %copy-start.88 = (f32[192]{0:T(256)S(1)}, f32[192]{0:T(256)}, u32[]{:S(2)}) copy-start(f32[192]{0:T(256)} %copy-done.87) | copy-start | bytes 2308
  719.5 201.5 %copy-start.90 = (f32[192]{0:T(256)S(1)}, f32[192]{0:T(256)}, u32[]{:S(2)}) copy-start(f32[192]{0:T(256)} %copy-done.89) | copy-start | bytes 2308
  719.5 203.1 %copy-start.100 = (f32[192]{0:T(256)S(1)}, f32[192]{0:T(256)}, u32[]{:S(2)}) copy-start(f32[192]{0:T(256)} %copy-done.99) | copy-start | bytes 2308
  719.6 203.1 %copy-start.98 = (f32[192]{0:T(256)S(1)}, f32[192]{0:T(256)}, u32[]{:S(2)}) copy-start(f32[192]{0:T(256)} %copy-done.97) | copy-start | bytes 2308
  719.6 356.1 %copy-start.80 = (f32[1024]{0:T(1024)S(1)}, f32[1024]{0:T(1024)}, u32[]{:S(2)}) copy-start(f32[1024]{0:T(1024)} %param.26) | copy-start | bytes 12292
  719.6 356.1 %copy-start.92 = (f32[192]{0:T(256)S(1)}, f32[192]{0:T(256)}, u32[]{:S(2)}) copy-start(f32[192]{0:T(256)} %copy-done.91) | copy-start | bytes 2308
  719.6 356.1 %copy-start.96 = (f32[192]{0:T(256)S(1)}, f32[192]{0:T(256)}, u32[]{:S(2)}) copy-start(f32[192]{0:T(256)} %copy-done.95) | copy-start | bytes 2308
  843.8 280.1 %copy-start.41 = (bf16[192,1024]{1,0:T(8,128)(2,1)S(1)}, bf16[192,1024]{1,0:T(8,128)(2,1)}, u32[]{:S(2)}) copy-start(bf16[192,1024]{1,0:T(8,128)(2,1)} %reduce-scatter.21.cloned.1.call-done) | copy-start | bytes 1179652
  1075.7 242.4 %copy-start.43 = (bf16[192,1024]{1,0:T(8,128)(2,1)S(1)}, bf16[192,1024]{1,0:T(8,128)(2,1)}, u32[]{:S(2)}) copy-start(bf16[192,1024]{1,0:T(8,128)(2,1)} %reduce-scatter.17.cloned.1.call-done) | copy-start | bytes 1179652
  1075.7 242.4 %copy-start.44 = (bf16[192,1024]{1,0:T(8,128)(2,1)S(1)}, bf16[192,1024]{1,0:T(8,128)(2,1)}, u32[]{:S(2)}) copy-start(bf16[192,1024]{1,0:T(8,128)(2,1)} %reduce-scatter.19.cloned.1.call-done) | copy-start | bytes 1179652
  (104 other events, 547.1 us)
Sparse Core Ops, SparseCore 0:
  10.2 100.8 all-gather.18
  113.3 117.6 all-gather.16
  232.5 15.5 all-gather.10
  250.1 60.0 all-gather.8
  312.2 58.9 all-gather.14
  372.6 15.3 all-gather.12
  620.5 22.3 reduce-scatter.28
  645.3 20.0 reduce-scatter.26
  667.8 20.0 reduce-scatter.24
  690.8 20.0 reduce-scatter.30
  713.5 24.8 reduce-scatter.32
  740.7 24.7 reduce-scatter.34
  769.1 74.6 reduce-scatter.20
  847.3 73.7 reduce-scatter.16
  924.5 73.8 reduce-scatter.18
  1001.8 73.7 reduce-scatter.22
  1079.1 118.1 reduce-scatter.14
  1200.7 117.2 reduce-scatter.12
